TPU v7x, 32 devices: a whole 2x2x4 slice. The times are simulated.
32 devices in a mesh: seq: 8 (over z, core), head: 4 (over y, x).
Axes of the slice: x: 2, y: 2, z: 4, core: 2. Of those that a mesh axis runs over, the one named last changes fastest.
Arguments:
- mixer_input: bfloat16 [2048, 4096], P('seq', 'head'), may hold values from -600 to 600
- gate_input: bfloat16 [2048, 4096], P('seq', 'head'), may hold values from -5 to 5
- b_proj: bfloat16 [2048, 128], P('seq'), may hold values from -0.5 to 0.5
- c_proj: bfloat16 [2048, 128], P('seq'), may hold values from -0.5 to 0.5
- decay_codes: int32 [64, 2048], P('head', 'seq'), may hold values from 1 to 4096
- decay_rates: float32 [64], P('head'), may hold values from 0 to 1
- skip_gain: float32 [64], P('head'), may hold values from 0.5 to 1.5
- norm_gain: float32 [4096], P('head'), may hold values from 0.5 to 1.5
- queries: bfloat16 [2048, 4096], P('seq', 'head'), may hold values from -5 to 5
- keys: bfloat16 [2048, 4096], P('seq', 'head'), may hold values from -5 to 5
Outputs:
- mamba_out: bfloat16 [2048, 4096], P('seq', 'head')
- attn_out: bfloat16 [2048, 4096], P('seq', 'head')
All inputs are finite; a program needn't handle non-finite values.
Results may differ from a plain program's by a relative error of at most 0.013.
Values may be sent and summed in bfloat16 or wider, within the bound.
No kernel may reach another device: no remote copies, remote signals or barrier semaphores. Data moves between devices by JAX's collectives and lax.ppermute only.
A program may use at most 64 MiB of HBM per device.

v0:
```python
import functools
import math
import jax
import jax.numpy as jnp
from jax import lax
from jax.sharding import PartitionSpec as P

HD = 128
CHANNELS_PER_HD = 64
BLOCK = 256
HIGH = lax.Precision.HIGHEST
NEG = -1e30


def carried_in(array, axis, combine, identity):
    devices, mine = (lax.axis_size(axis), lax.axis_index(axis))
    everything = jax.tree.map(
        lambda part, kind: lax.all_gather(part.astype(kind), axis),
        array,
        (jnp.bfloat16, jnp.bfloat16),
    )
    start = jax.tree.map(
        lambda part, zero: jnp.broadcast_to(jnp.asarray(zero, part.dtype), part.shape),
        array,
        identity,
    )

    def hop(k, before):
        reached = k < mine
        new = combine(
            before, jax.tree.map(lambda part, own: part[k].astype(own.dtype), everything, array)
        )
        return jax.tree.map(lambda a, b: jnp.where(reached, a, b), new, before)

    return lax.fori_loop(0, devices, hop, start)


def block_step(state_carry, inputs):
    x_block, b_block, c_block, decay_block = inputs
    running = jnp.cumsum(decay_block, axis=1)
    span = decay_block.shape[1]
    causal = (
        jnp.arange(span, dtype=jnp.int32)[:, None] >= jnp.arange(span, dtype=jnp.int32)[None, :]
    )
    log_gaps = jnp.where(causal[None, :, :], running[:, :, None] - running[:, None, :], NEG)
    decays = jnp.exp(log_gaps)
    match_strength = jnp.dot(c_block, b_block.T, preferred_element_type=jnp.float32)
    x_float = x_block.astype(jnp.float32)
    within = jnp.einsum(
        "hts,shp->thp", decays * match_strength[None, :, :], x_float, precision=HIGH
    )
    c_float = c_block.astype(jnp.float32)
    carried = jnp.exp(running).T[:, :, None] * jnp.einsum(
        "tn,hnp->thp", c_float, state_carry, precision=HIGH
    )
    to_end = jnp.exp(running[:, -1:] - running)
    updated_state = jnp.exp(running[:, -1])[:, None, None] * state_carry + jnp.einsum(
        "hs,sn,shp->hnp", to_end, b_block.astype(jnp.float32), x_float, precision=HIGH
    )
    return (updated_state, within + carried)


def local_scan(x_local, b_local, c_local, log_decay):
    tok_rows = x_local.shape[0]
    heads_local = log_decay.shape[0]
    block_count = tok_rows // BLOCK
    x_blocks = x_local.reshape(block_count, BLOCK, heads_local, CHANNELS_PER_HD)
    b_blocks = b_local.reshape(block_count, BLOCK, b_local.shape[1])
    c_blocks = c_local.reshape(block_count, BLOCK, c_local.shape[1])
    decay_blocks = log_decay.reshape(heads_local, block_count, BLOCK).transpose(1, 0, 2)
    initial = jnp.zeros((heads_local, b_local.shape[1], CHANNELS_PER_HD), jnp.float32)
    final_state, y_blocks = lax.scan(
        block_step, initial, (x_blocks, b_blocks, c_blocks, decay_blocks)
    )
    return (final_state, y_blocks.reshape(tok_rows, heads_local, CHANNELS_PER_HD))


def masked_scores(q_rows, q_pos, k_rows, k_pos):
    score_scale = 1.0 / math.sqrt(k_rows.shape[-1])
    scores = (
        jnp.einsum("qhd,khd->hqk", q_rows, k_rows, preferred_element_type=jnp.float32) * score_scale
    )
    visible = k_pos[None, None, :] <= q_pos[None, :, None]
    return (jnp.where(visible, scores, NEG), visible)


def online_update(group_state, q_rows, q_pos, k_rows, v_rows, k_pos):
    row_top, row_total, weighted_sum = group_state
    scores, visible = masked_scores(q_rows, q_pos, k_rows, k_pos)
    new_top = jnp.maximum(row_top, jnp.max(scores, axis=2))
    rescale = jnp.exp(row_top - new_top)
    weights = jnp.where(visible, jnp.exp(scores - new_top[:, :, None]), 0.0)
    row_total = row_total * rescale + jnp.sum(weights, axis=2)
    weighted_sum = weighted_sum * rescale[:, :, None] + jnp.einsum(
        "hqk,khd->hqd", weights.astype(jnp.bfloat16), v_rows, preferred_element_type=jnp.float32
    )
    return (new_top, row_total, weighted_sum)


def when_visible(state_update, group_state, q_pos, key_offset):
    return lax.cond(key_offset > q_pos[-1], lambda held: held, state_update, group_state)


def on_device(
    mixer_input,
    gate_input,
    b_proj,
    c_proj,
    decay_codes,
    decay_rates,
    skip_gain,
    norm_gain,
    queries,
    keys,
):
    tok_rows = mixer_input.shape[0]
    heads_local = decay_rates.shape[0]
    heads_att = queries.shape[1] // HD
    seq_rank = lax.axis_index("seq")
    own_positions = seq_rank * tok_rows + jnp.arange(tok_rows, dtype=jnp.int32)
    groups = [(queries, own_positions)]
    groups = [(q_rows.reshape(q_rows.shape[0], heads_att, HD), q_pos) for q_rows, q_pos in groups]
    log_decay = -decay_rates[:, None] * decay_codes.astype(jnp.float32)
    local_state, y_local = local_scan(mixer_input, b_proj, c_proj, log_decay)
    total_log = jnp.sum(log_decay, axis=1)

    def combine(earlier, later):
        return (earlier[0] + later[0], jnp.exp(later[0])[:, None, None] * earlier[1] + later[1])

    identity = (jnp.zeros_like(total_log), jnp.zeros_like(local_state))
    _, incoming = carried_in((total_log, local_state), "seq", combine, identity)
    running = jnp.cumsum(log_decay, axis=1)
    carried = jnp.einsum("tn,hnp->thp", c_proj.astype(jnp.float32), incoming, precision=HIGH)
    carried = carried * jnp.exp(running).T[:, :, None]
    x_float = mixer_input.reshape(tok_rows, heads_local, CHANNELS_PER_HD).astype(jnp.float32)
    ssm_out = (y_local + carried + skip_gain[None, :, None] * x_float).reshape(
        tok_rows, heads_local * CHANNELS_PER_HD
    )
    gated = ssm_out * jax.nn.silu(gate_input.astype(jnp.float32))
    squares = lax.psum(jnp.sum(gated * gated, axis=1), "head")
    channels = gated.shape[1] * lax.axis_size("head")
    mamba_out = (
        gated * lax.rsqrt(squares / channels + 1e-05)[:, None] * norm_gain[None, :]
    ).astype(jnp.bfloat16)
    initial = tuple(
        (
            (
                jnp.full((heads_att, q_pos.shape[0]), NEG, jnp.float32),
                jnp.zeros((heads_att, q_pos.shape[0]), jnp.float32),
                jnp.zeros((heads_att, q_pos.shape[0], HD), jnp.float32),
            )
            for _, q_pos in groups
        )
    )
    states = initial
    k_piece = lax.all_gather(keys, "seq", axis=0, tiled=True)
    v_piece = lax.all_gather(mamba_out, "seq", axis=0, tiled=True)
    row_count = k_piece.shape[0]
    block_rows = math.gcd(row_count, 512)

    def one_block(block_id, states):
        key_offset = block_id * block_rows
        k_rows = lax.dynamic_slice_in_dim(k_piece, block_id * block_rows, block_rows, 0).reshape(
            block_rows, heads_att, HD
        )
        v_rows = lax.dynamic_slice_in_dim(v_piece, block_id * block_rows, block_rows, 0).reshape(
            block_rows, heads_att, HD
        )
        k_pos = key_offset + jnp.arange(block_rows, dtype=jnp.int32)
        return tuple(
            (
                when_visible(
                    functools.partial(
                        online_update,
                        q_rows=group[0],
                        q_pos=group[1],
                        k_rows=k_rows,
                        v_rows=v_rows,
                        k_pos=k_pos,
                    ),
                    group_state,
                    group[1],
                    key_offset,
                )
                for group, group_state in zip(groups, states)
            )
        )

    finals = lax.fori_loop(0, row_count // block_rows, one_block, states)
    results = [(group_state[2], group_state[1]) for group_state in finals]
    rows_out = [
        (weighted / totals[:, :, None])
        .transpose(1, 0, 2)
        .reshape(weighted.shape[1], heads_att * HD)
        .astype(jnp.bfloat16)
        for weighted, totals in results
    ]
    attn_out = rows_out[0]
    return (mamba_out, attn_out)


def solution(mesh):
    in_specs = (
        P("seq", "head"),
        P("seq", "head"),
        P("seq", None),
        P("seq", None),
        P("head", "seq"),
        P("head"),
        P("head"),
        P("head"),
        P("seq", "head"),
        P("seq", "head"),
    )
    out_specs = (P("seq", "head"), P("seq", "head"))
    return jax.shard_map(
        on_device, mesh=mesh, in_specs=in_specs, out_specs=out_specs, check_vma=False
    )
```

profile of v0, /device:TPU:25, one launch (start us, length us, event | category | flops | bytes accessed | tf_op | source)
XLA Modules:
  0.0 200.4 jit_solution(12899004294406485471)
XLA Ops:
  7.2 0.7 neg.8
  7.9 0.9 fusion.43
  8.8 0.6 reduce-window.12
  9.9 1.2 copy.56
  11.2 2.2 %fusion.32 = bf16[16,128,64]{1,2,0:T(8,128)(2,1)} fusion(bf16[256,16,64]{0,2,1:T(8,128)(2,1)S(1)} %bitcast.92, f32[256,16]{0,1:T(8,128)S(1)} %get-tuple-element.482, f32[16]{0:T(128)S(1)} %exponential_multiply_fusion, bf16[256,128]{1,0:T(8,128)(2,1)} %param.18), kind=kOutput, calls=%fused_computation.45 | convolution fusion | flops 403439616 | bytes 868416 | tf_op jit(solution)/shard_map/while/body/eval_jaxpr/hs,sn,shp->hnp/dot_general | solution.py:57
  13.5 1.3 dynamic-slice.3
  15.6 13.3 %all-reduce = bf16[128]{0:T(256)(128)(2,1)S(1)} all-reduce(bf16[128]{0:T(256)(128)(2,1)S(1)} %dynamic-update-slice), channel_id=2, replica_groups=mesh['seq'=8,'head'=4] {'seq'}, use_global_device_ids=true, to_apply=%add | all-reduce | flops 128 | bytes 512
  29.1 1.0 fusion.47
  30.1 3.0 %fusion.23 = f32[256,16,64]{0,2,1:T(8,128)S(1)} fusion(bf16[256,16,64]{0,2,1:T(8,128)(2,1)S(1)} %bitcast.93, f32[256,256]{1,0:T(8,128)S(1)} %fusion.47, f32[16,256]{1,0:T(8,128)S(1)} %copy_bitcast_fusion.1, pred[256,256]{1,0:T(8,128)(4,1)S(1)} %iota_compare_fusion), kind=kOutput, calls=%fused_computation.32 | convolution fusion | flops 808452096 | bytes 1916928 | tf_op jit(solution)/shard_map/while/body/eval_jaxpr/hts,shp->thp/dot_general | solution.py:49
  33.1 0.6 fusion.30
  33.7 9.1 %all-gather.10.cloned.1.call-done = bf16[128,128,64]{1,2,0:T(8,128)(2,1)} async-done(((bf16[16,128,64]{1,2,0:T(8,128)(2,1)}), bf16[128,128,64]{1,2,0:T(8,128)(2,1)}) %all-gather.10.cloned.1.call-update) | async-done | bytes 2097168 | tf_op jit(solution)/shard_map/all_gather | solution.py:18
  42.8 13.6 %while.37 = (s32[]{:T(128)}, f32[16,128,64]{2,1,0:T(8,128)S(1)}, s32[]{:T(128)}, bf16[8,16]{1,0:T(8,128)(2,1)S(1)}, bf16[8,16,128,64]{2,3,1,0:T(8,128)(2,1)}, /*index=5*/s32[]{:T(128)}, s32[]{:T(128)}) while((s32[]{:T(128)}, f32[16,128,64]{2,1,0:T(8,128)S(1)}, s32[]{:T(128)}, bf16[8,16]{1,0:T(8,128)(2,1)S(1)}, ...), condition=%wide.region_4.5_spmd.clone, body=%wide.region_3.4_spmd.clone.sunk | while | flops 655380 | bytes 2359569 | solution.py:35
  42.8 1.0 constant_dynamic-slice_fusion.4
  43.8 0.3 copy.82
  44.1 0.4 fusion.57
  44.5 1.0 constant_dynamic-slice_fusion.4
  45.8 0.4 fusion.57
  46.2 1.0 constant_dynamic-slice_fusion.4
  47.5 0.4 fusion.57
  47.9 1.0 constant_dynamic-slice_fusion.4
  49.2 0.4 fusion.57
  49.6 1.0 constant_dynamic-slice_fusion.4
  50.9 0.4 fusion.57
  51.3 1.0 constant_dynamic-slice_fusion.4
  52.6 0.4 fusion.57
  53.0 1.0 constant_dynamic-slice_fusion.4
  54.3 0.4 fusion.57
  54.7 1.0 constant_dynamic-slice_fusion.4
  56.0 0.4 fusion.57
  56.4 2.1 %fusion.28 = f32[256,16,64]{0,2,1:T(8,128)} fusion(f32[256,16,64]{0,2,1:T(8,128)S(1)} %fusion.30, f32[16,128,64]{2,1,0:T(8,128)S(1)} %get-tuple-element.383, bf16[256,16,64]{0,2,1:T(8,128)(2,1)S(1)} %bitcast.94, f32[16]{0:T(128)S(1)} %copy-done.5, f32[256,16]{0,1:T(8,128)S(1)} %get-tuple-element.483, bf16[256,128]{1,0:T(8,128)(2,1)S(1)} %copy-done), kind=kOutput, calls=%fused_computation.36 | convolution fusion | flops 403963904 | bytes 3227712 | tf_op jit(solution)/shard_map/tn,hnp->thp/dot_general | solution.py:133
  58.5 1.6 copy.59
  60.2 0.4 multiply_reduce_fusion
  60.6 7.8 %psum.7 = f32[256]{0:T(256)S(1)} all-reduce(f32[256]{0:T(256)S(1)} %multiply_reduce_fusion), channel_id=1, replica_groups=mesh['seq'=8,'head'=4] {'head'}, use_global_device_ids=true, to_apply=%region_6.7 | all-reduce | flops 256 | bytes 2048 | tf_op jit(solution)/shard_map/psum | solution.py:140
  68.3 1.2 multiply_convert_fusion
  69.8 1.0 copy.60
  71.3 44.5 %all-gather.8.cloned.1.call-done = bf16[2048,1024]{1,0:T(8,128)(2,1)} async-done(((bf16[256,1024]{1,0:T(8,128)(2,1)}), bf16[2048,1024]{1,0:T(8,128)(2,1)}) %all-gather.8.cloned.1.call-update) | async-done | bytes 4194320 | tf_op jit(solution)/shard_map/all_gather | solution.py:157
  115.8 6.5 %copy.63 = bf16[2048,1024]{0,1:T(8,128)(2,1)} copy(bf16[2048,1024]{1,0:T(8,128)(2,1)} %all-gather.8.cloned.1.call-done) | data formatting | bytes 8388608 | tf_op jit(solution)/shard_map/while | solution.py:189
  122.3 41.8 %all-gather.6.cloned.1.call-done = bf16[2048,1024]{0,1:T(8,128)(2,1)} async-done(((bf16[256,1024]{0,1:T(8,128)(2,1)}), bf16[2048,1024]{0,1:T(8,128)(2,1)}) %all-gather.6.cloned.1.call-update) | async-done | bytes 4194320 | tf_op jit(solution)/shard_map/all_gather | solution.py:156
  164.2 28.6 %while.36 = (s32[]{:T(128)}, f32[8,256]{1,0:T(8,128)S(1)}, f32[8,256]{1,0:T(8,128)S(1)}, f32[8,256,128]{2,1,0:T(8,128)S(1)}, s32[256]{0:T(256)S(1)}, /*index=5*/...) while((s32[]{:T(128)}, f32[8,256]{1,0:T(8,128)S(1)}, ...), condition=%wide.region_12.13_spmd, body=%wide.region_7.12_spmd.sunk | while | flops 551162368 | bytes 22160680 | solution.py:189
  164.2 0.6 slice.28
  165.3 6.0 %conditional.2 = (f32[8,256]{1,0:T(8,128)S(1)}, f32[8,256]{1,0:T(8,128)S(1)}, f32[8,256,128]{2,1,0:T(8,128)S(1)}) conditional(s32[]{:T(128)} %convert_element_type.129, (s32[]{:T(128)}, s32[512]{0:T(512)S(1)}, s32[256]{0:T(256)S(1)}, bf16[2048,1024]{0,1:T(8,128)(2,1)}, bf16[256,8,128]{2,0,1:T(8,128)(2,1)S(1)}, /*index=5*/f32[8,256]{1,0:T(8,128)S(1)}, ...), branch_computations={%region_8.10_spmd, %region_11.11_spmd} | conditional | flops 551162368 | bytes 22142018 | solution.py:101
  165.5 1.7 constant_dynamic-slice_fusion
  167.2 0.9 fusion
  168.2 1.0 fusion.2
  169.2 2.1 %fusion.6 = f32[8,256,128]{2,1,0:T(8,128)S(1)} fusion(bf16[512,8,128]{0,2,1:T(8,128)(2,1)S(1)} %bitcast.91, f32[8,512,256]{2,1,0:T(8,128)S(1)} %get-tuple-element.477, f32[8,256]{1,0:T(8,128)S(1)} %max.5, pred[256,512]{0,1:T(8,128)(4,1)S(1)} %broadcast_compare_fusion, f32[8,256,128]{2,1,0:T(8,128)S(1)} %get-tuple-element.364, ...), kind=kOutput, calls=%fused_computation.7 | convolution fusion | flops 274202624 | bytes 7487488 | tf_op jit(solution)/shard_map/while/body/eval_jaxpr/cond/branch_0_fun/hqk,khd->hqd/dot_general | solution.py:94
  171.3 0.6 slice.28
  172.5 6.0 %conditional.2 = (f32[8,256]{1,0:T(8,128)S(1)}, f32[8,256]{1,0:T(8,128)S(1)}, f32[8,256,128]{2,1,0:T(8,128)S(1)}) conditional(s32[]{:T(128)} %convert_element_type.129, (s32[]{:T(128)}, s32[512]{0:T(512)S(1)}, s32[256]{0:T(256)S(1)}, bf16[2048,1024]{0,1:T(8,128)(2,1)}, bf16[256,8,128]{2,0,1:T(8,128)(2,1)S(1)}, /*index=5*/f32[8,256]{1,0:T(8,128)S(1)}, ...), branch_computations={%region_8.10_spmd, %region_11.11_spmd} | conditional | flops 551162368 | bytes 22142018 | solution.py:101
  172.7 1.7 constant_dynamic-slice_fusion
  174.4 0.9 fusion
  175.3 1.0 fusion.2
  176.3 2.1 %fusion.6 = f32[8,256,128]{2,1,0:T(8,128)S(1)} fusion(bf16[512,8,128]{0,2,1:T(8,128)(2,1)S(1)} %bitcast.91, f32[8,512,256]{2,1,0:T(8,128)S(1)} %get-tuple-element.477, f32[8,256]{1,0:T(8,128)S(1)} %max.5, pred[256,512]{0,1:T(8,128)(4,1)S(1)} %broadcast_compare_fusion, f32[8,256,128]{2,1,0:T(8,128)S(1)} %get-tuple-element.364, ...), kind=kOutput, calls=%fused_computation.7 | convolution fusion | flops 274202624 | bytes 7487488 | tf_op jit(solution)/shard_map/while/body/eval_jaxpr/cond/branch_0_fun/hqk,khd->hqd/dot_general | solution.py:94
  178.5 0.6 slice.28
  179.6 6.0 %conditional.2 = (f32[8,256]{1,0:T(8,128)S(1)}, f32[8,256]{1,0:T(8,128)S(1)}, f32[8,256,128]{2,1,0:T(8,128)S(1)}) conditional(s32[]{:T(128)} %convert_element_type.129, (s32[]{:T(128)}, s32[512]{0:T(512)S(1)}, s32[256]{0:T(256)S(1)}, bf16[2048,1024]{0,1:T(8,128)(2,1)}, bf16[256,8,128]{2,0,1:T(8,128)(2,1)S(1)}, /*index=5*/f32[8,256]{1,0:T(8,128)S(1)}, ...), branch_computations={%region_8.10_spmd, %region_11.11_spmd} | conditional | flops 551162368 | bytes 22142018 | solution.py:101
  179.8 1.7 constant_dynamic-slice_fusion
  181.5 0.9 fusion
  182.5 1.0 fusion.2
  183.5 2.1 %fusion.6 = f32[8,256,128]{2,1,0:T(8,128)S(1)} fusion(bf16[512,8,128]{0,2,1:T(8,128)(2,1)S(1)} %bitcast.91, f32[8,512,256]{2,1,0:T(8,128)S(1)} %get-tuple-element.477, f32[8,256]{1,0:T(8,128)S(1)} %max.5, pred[256,512]{0,1:T(8,128)(4,1)S(1)} %broadcast_compare_fusion, f32[8,256,128]{2,1,0:T(8,128)S(1)} %get-tuple-element.364, ...), kind=kOutput, calls=%fused_computation.7 | convolution fusion | flops 274202624 | bytes 7487488 | tf_op jit(solution)/shard_map/while/body/eval_jaxpr/cond/branch_0_fun/hqk,khd->hqd/dot_general | solution.py:94
  185.6 0.6 slice.28
  186.8 6.0 %conditional.2 = (f32[8,256]{1,0:T(8,128)S(1)}, f32[8,256]{1,0:T(8,128)S(1)}, f32[8,256,128]{2,1,0:T(8,128)S(1)}) conditional(s32[]{:T(128)} %convert_element_type.129, (s32[]{:T(128)}, s32[512]{0:T(512)S(1)}, s32[256]{0:T(256)S(1)}, bf16[2048,1024]{0,1:T(8,128)(2,1)}, bf16[256,8,128]{2,0,1:T(8,128)(2,1)S(1)}, /*index=5*/f32[8,256]{1,0:T(8,128)S(1)}, ...), branch_computations={%region_8.10_spmd, %region_11.11_spmd} | conditional | flops 551162368 | bytes 22142018 | solution.py:101
  187.0 1.7 constant_dynamic-slice_fusion
  188.7 0.9 fusion
  189.6 1.0 fusion.2
  190.6 2.1 %fusion.6 = f32[8,256,128]{2,1,0:T(8,128)S(1)} fusion(bf16[512,8,128]{0,2,1:T(8,128)(2,1)S(1)} %bitcast.91, f32[8,512,256]{2,1,0:T(8,128)S(1)} %get-tuple-element.477, f32[8,256]{1,0:T(8,128)S(1)} %max.5, pred[256,512]{0,1:T(8,128)(4,1)S(1)} %broadcast_compare_fusion, f32[8,256,128]{2,1,0:T(8,128)S(1)} %get-tuple-element.364, ...), kind=kOutput, calls=%fused_computation.7 | convolution fusion | flops 274202624 | bytes 7487488 | tf_op jit(solution)/shard_map/while/body/eval_jaxpr/cond/branch_0_fun/hqk,khd->hqd/dot_general | solution.py:94
  192.8 1.1 copy_bitcast_fusion
  (77 shorter events, 4.6 us)
Async XLA Ops:
  7.2 21.9 %copy-start = (bf16[256,128]{1,0:T(8,128)(2,1)S(1)}, bf16[256,128]{1,0:T(8,128)(2,1)}, u32[]{:S(2)}) copy-start(bf16[256,128]{1,0:T(8,128)(2,1)} %param.19) | copy-start | bytes 196612
  7.2 35.6 %all-gather.10.cloned.1.call-start = ((), (), s32[]{:S(2)}) async-start(), calls=%async_computation.2 | async-start | bytes 2359296 | tf_op jit(solution)/shard_map/all_gather | solution.py:18
  13.4 102.4 %all-gather.8.cloned.1.call-start = ((), (), s32[]{:S(2)}) async-start(), calls=%async_computation.1 | async-start | bytes 4718592 | tf_op jit(solution)/shard_map/all_gather | solution.py:157
  42.8 13.6 %copy-start.5 = (f32[16]{0:T(128)S(1)}, f32[16]{0:T(128)}, u32[]{:S(2)}) copy-start(f32[16]{0:T(128)} %param.22) | copy-start | bytes 196
  56.4 3.8 %copy-start.1 = (bf16[256,1024]{1,0:T(8,128)(2,1)S(1)}, bf16[256,1024]{1,0:T(8,128)(2,1)}, u32[]{:S(2)}) copy-start(bf16[256,1024]{1,0:T(8,128)(2,1)} %param.17) | copy-start | bytes 1572868
  56.4 12.0 %copy-start.4 = (f32[1024]{0:T(1024)S(1)}, f32[1024]{0:T(1024)}, u32[]{:S(2)}) copy-start(f32[1024]{0:T(1024)} %param.23) | copy-start | bytes 12292
  58.5 11.3 %copy-start.2 = (bf16[256,1024]{1,0:T(8,128)(2,1)S(1)}, bf16[256,1024]{1,0:T(8,128)(2,1)}, u32[]{:S(2)}) copy-start(bf16[256,1024]{1,0:T(8,128)(2,1)} %param.25) | copy-start | bytes 1572868
  58.5 12.3 %copy-start.3 = (bf16[256,1024]{1,0:T(8,128)(2,1)S(1)}, bf16[256,1024]{1,0:T(8,128)(2,1)}, u32[]{:S(2)}) copy-start(bf16[256,1024]{1,0:T(8,128)(2,1)} %param.24) | copy-start | bytes 1572868
  69.5 94.6 %all-gather.6.cloned.1.call-start = ((), (), s32[]{:S(2)}) async-start(), calls=%async_computation | async-start | bytes 4718592 | tf_op jit(solution)/shard_map/all_gather | solution.py:156
Sparse Core Ops, SparseCore 0:
  13.5 29.2 all-gather.9
  69.7 46.0 all-gather.7
  118.0 46.0 all-gather.5
where the time goes:
time: 201 us; the launch traced here: 200 us
  waiting for transfers between devices  95.4 us (47%)
  local copies, waits for them, and re-layouts  32 us (16%)
  blocking collectives  21.1 us (10%)
  matrix products  21 us (10%)
  between operations  14.6 us (7%)
  other arithmetic  12.9 us (6%)
  loops' own time  3.13 us (2%)
    all_gather x1, waiting for transfers between devices, on_device(): v_piece = lax.all_gather(mamba_out, 'seq', axis=0, tiled=True)  44.5 us
    all_gather x1, waiting for transfers between devices, on_device(): k_piece = lax.all_gather(keys, 'seq', axis=0, tiled=True)  41.8 us
    unnamed x1, blocking collectives  13.3 us
    dynamic_slice x16, local copies, waits for them, and re-layouts, hop(): part[k].astype(own.dtype)  10.1 us
    all_gather x1, waiting for transfers between devices, carried_in(): lax.all_gather(part.astype(kind), axis)  9.1 us
    dot_general x4, matrix products, online_update(): jnp.einsum('hqk,khd->hqd', weights.astype(jnp.bfloat16), v_rows, preferre...  8.4 us
    psum x1, blocking collectives, on_device(): squares = lax.psum(jnp.sum(gated * gated, axis=1), 'head')  7.76 us
    while x2, local copies, waits for them, and re-layouts, on_device(): finals = lax.fori_loop(0, row_count // block_rows, one_block, states)  6.79 us
  transfers between devices with their start and end apart: 3, of which 3 were waited for; matrix products, arithmetic and copies ran while one was open for 7% of the time, Pallas kernels for 0%

commit v1 on v0

--- a/solution.py
+++ b/solution.py
@@ -4,12 +4,18 @@
 import jax.numpy as jnp
 from jax import lax
 from jax.sharding import PartitionSpec as P
+from jax.lax import all_gather
 
 HD = 128
 CHANNELS_PER_HD = 64
 BLOCK = 256
 HIGH = lax.Precision.HIGHEST
 NEG = -1e30
+create_numbers_on = lambda chunk, block_here: jnp.split(
+    all_gather(jnp.concatenate([chunk, block_here], axis=1), "seq", axis=0, tiled=True),
+    [chunk.shape[1]],
+    axis=1,
+)
 
 
 def carried_in(array, axis, combine, identity):
@@ -153,8 +159,7 @@
         )
     )
     states = initial
-    k_piece = lax.all_gather(keys, "seq", axis=0, tiled=True)
-    v_piece = lax.all_gather(mamba_out, "seq", axis=0, tiled=True)
+    k_piece, v_piece = create_numbers_on(keys, mamba_out)
     row_count = k_piece.shape[0]
     block_rows = math.gcd(row_count, 512)
 

time: 201 us -> 208 us (1.035)
  local copies, waits for them, and re-layouts: 32 us -> 43.4 us
  waiting for transfers between devices: 95.4 us -> 89.2 us
    while x2 -> x3, local copies, waits for them, and re-layouts: 6.79 us -> 13.3 us  [on_device(): finals = lax.fori_loop(0, row_count // block_rows, one_block, states)]
    all_gather x2 -> x1, waiting for transfers between devices: 86.3 us -> 80.1 us  [all_gather(jnp.concatenate([chunk, block_here], axis=1), 'seq', axis=0, t...]
    split x0 -> x1, local copies, waits for them, and re-layouts: none -> 5.9 us  [jnp.split(all_gather(jnp.concatenate([chunk, block_here], axis=1), 'seq',...]
  transfers between devices with their start and end apart: 3 -> 2, of which waited for: 3 -> 2; matrix products, arithmetic and copies ran while one was open for 7% -> 3% of each run, Pallas kernels for 0% -> 0%
where the time goes in v1:
time: 208 us; the launch traced here: 206 us
  waiting for transfers between devices  89.2 us (43%)
  local copies, waits for them, and re-layouts  43.4 us (21%)
  blocking collectives  21.3 us (10%)
  matrix products  21 us (10%)
  between operations  14.9 us (7%)
  other arithmetic  13.4 us (6%)
  loops' own time  3.12 us (2%)
    all_gather x1, waiting for transfers between devices, all_gather(jnp.concatenate([chunk, block_here], axis=1), 'seq', axis=0, t...  80.1 us
    unnamed x1, blocking collectives  13.3 us
    while x3, local copies, waits for them, and re-layouts, on_device(): finals = lax.fori_loop(0, row_count // block_rows, one_block, states)  13.3 us
    dynamic_slice x16, local copies, waits for them, and re-layouts, hop(): part[k].astype(own.dtype)  10.1 us
    all_gather x1, waiting for transfers between devices, carried_in(): lax.all_gather(part.astype(kind), axis)  9.09 us
    dot_general x4, matrix products, online_update(): jnp.einsum('hqk,khd->hqd', weights.astype(jnp.bfloat16), v_rows, preferre...  8.4 us
    psum x1, blocking collectives, on_device(): squares = lax.psum(jnp.sum(gated * gated, axis=1), 'head')  7.94 us
    dynamic_slice x4, local copies, waits for them, and re-layouts, one_block(): lax.dynamic_slice_in_dim(v_piece, block_id * block_rows, block_rows, 0)  6.76 us
  transfers between devices with their start and end apart: 2, of which 2 were waited for; matrix products, arithmetic and copies ran while one was open for 3% of the time, Pallas kernels for 0%

profile of v1, /device:TPU:25, one launch (start us, length us, event | category | flops | bytes accessed | tf_op | source)
XLA Modules:
  0.0 206.4 jit_solution(3087493953639364013)
XLA Ops:
  7.2 0.7 neg.8
  7.9 0.9 fusion.43
  8.8 0.6 reduce-window.12
  9.9 1.2 copy.56
  11.2 2.2 %fusion.32 = bf16[16,128,64]{1,2,0:T(8,128)(2,1)} fusion(bf16[256,16,64]{0,2,1:T(8,128)(2,1)S(1)} %bitcast.92, f32[256,16]{0,1:T(8,128)S(1)} %get-tuple-element.484, f32[16]{0:T(128)S(1)} %exponential_multiply_fusion, bf16[256,128]{1,0:T(8,128)(2,1)} %param.18), kind=kOutput, calls=%fused_computation.45 | convolution fusion | flops 403439616 | bytes 868416 | tf_op jit(solution)/shard_map/while/body/eval_jaxpr/hs,sn,shp->hnp/dot_general | solution.py:63
  13.5 1.2 dynamic-slice.3
  15.7 13.3 %all-reduce = bf16[128]{0:T(256)(128)(2,1)S(1)} all-reduce(bf16[128]{0:T(256)(128)(2,1)S(1)} %dynamic-update-slice), channel_id=2, replica_groups=mesh['seq'=8,'head'=4] {'seq'}, use_global_device_ids=true, to_apply=%add | all-reduce | flops 128 | bytes 512
  29.1 1.0 fusion.48
  30.1 3.0 %fusion.23 = f32[256,16,64]{0,2,1:T(8,128)S(1)} fusion(bf16[256,16,64]{0,2,1:T(8,128)(2,1)S(1)} %bitcast.93, f32[256,256]{1,0:T(8,128)S(1)} %fusion.48, f32[16,256]{1,0:T(8,128)S(1)} %copy_bitcast_fusion.1, pred[256,256]{1,0:T(8,128)(4,1)S(1)} %iota_compare_fusion), kind=kOutput, calls=%fused_computation.32 | convolution fusion | flops 808452096 | bytes 1916928 | tf_op jit(solution)/shard_map/while/body/eval_jaxpr/hts,shp->thp/dot_general | solution.py:55
  33.1 0.6 fusion.30
  33.7 9.1 %all-gather.7.cloned.1.call-done = bf16[128,128,64]{1,2,0:T(8,128)(2,1)} async-done(((bf16[16,128,64]{1,2,0:T(8,128)(2,1)}), bf16[128,128,64]{1,2,0:T(8,128)(2,1)}) %all-gather.7.cloned.1.call-update) | async-done | bytes 2097168 | tf_op jit(solution)/shard_map/all_gather | solution.py:24
  42.8 13.5 %while.37 = (s32[]{:T(128)}, f32[16,128,64]{2,1,0:T(8,128)S(1)}, s32[]{:T(128)}, bf16[8,16]{1,0:T(8,128)(2,1)S(1)}, bf16[8,16,128,64]{2,3,1,0:T(8,128)(2,1)}, /*index=5*/s32[]{:T(128)}, s32[]{:T(128)}) while((s32[]{:T(128)}, f32[16,128,64]{2,1,0:T(8,128)S(1)}, s32[]{:T(128)}, bf16[8,16]{1,0:T(8,128)(2,1)S(1)}, ...), condition=%wide.region_4.5_spmd.clone, body=%wide.region_3.4_spmd.clone.sunk | while | flops 655380 | bytes 2359561 | solution.py:41
  42.8 1.0 constant_dynamic-slice_fusion.4
  44.1 0.4 fusion.58
  44.5 1.0 constant_dynamic-slice_fusion.4
  45.8 0.4 fusion.58
  46.2 1.0 constant_dynamic-slice_fusion.4
  47.5 0.4 fusion.58
  47.9 1.0 constant_dynamic-slice_fusion.4
  49.2 0.4 fusion.58
  49.6 1.0 constant_dynamic-slice_fusion.4
  50.9 0.4 fusion.58
  51.3 1.0 constant_dynamic-slice_fusion.4
  52.6 0.4 fusion.58
  53.0 1.0 constant_dynamic-slice_fusion.4
  54.3 0.4 fusion.58
  54.7 1.0 constant_dynamic-slice_fusion.4
  56.0 0.4 fusion.58
  56.4 2.1 %fusion.28 = f32[256,16,64]{0,2,1:T(8,128)} fusion(f32[256,16,64]{0,2,1:T(8,128)S(1)} %fusion.30, f32[16,128,64]{2,1,0:T(8,128)S(1)} %get-tuple-element.383, bf16[256,16,64]{0,2,1:T(8,128)(2,1)S(1)} %bitcast.94, f32[16]{0:T(128)S(1)} %copy-done.6, f32[256,16]{0,1:T(8,128)S(1)} %get-tuple-element.485, bf16[256,128]{1,0:T(8,128)(2,1)S(1)} %copy-done), kind=kOutput, calls=%fused_computation.36 | convolution fusion | flops 403963904 | bytes 3227712 | tf_op jit(solution)/shard_map/tn,hnp->thp/dot_general | solution.py:139
  58.5 1.6 copy.59
  60.2 0.4 multiply_reduce_fusion
  60.6 7.9 %psum.7 = f32[256]{0:T(256)S(1)} all-reduce(f32[256]{0:T(256)S(1)} %multiply_reduce_fusion), channel_id=1, replica_groups=mesh['seq'=8,'head'=4] {'head'}, use_global_device_ids=true, to_apply=%region_6.7 | all-reduce | flops 256 | bytes 2048 | tf_op jit(solution)/shard_map/psum | solution.py:146
  68.5 0.4 multiply_convert_fusion
  68.9 1.2 pad_maximum_fusion
  70.7 80.1 %all-gather.5.cloned.1.call-done = bf16[2048,2048]{1,0:T(8,128)(2,1)} async-done(((bf16[256,2048]{1,0:T(8,128)(2,1)}), bf16[2048,2048]{1,0:T(8,128)(2,1)}) %all-gather.5.cloned.1.call-update) | async-done | bytes 8388624 | tf_op jit(solution)/shard_map/all_gather | solution.py:15
  150.8 5.9 %fusion.47 = (bf16[2048,1024]{1,0:T(8,128)(2,1)}, bf16[2048,1024]{1,0:T(8,128)(2,1)}) fusion(bf16[2048,2048]{1,0:T(8,128)(2,1)} %all-gather.5.cloned.1.call-done), kind=kLoop, calls=%fused_computation.77 | loop fusion | bytes 16777216 | tf_op jit(solution)/shard_map/split | solution.py:14
  156.7 6.5 %copy.61 = bf16[2048,1024]{0,1:T(8,128)(2,1)} copy(bf16[2048,1024]{1,0:T(8,128)(2,1)} %get-tuple-element.481) | data formatting | bytes 8388608 | tf_op jit(solution)/shard_map/while | solution.py:194
  163.2 6.5 %copy.63 = bf16[2048,1024]{0,1:T(8,128)(2,1)} copy(bf16[2048,1024]{1,0:T(8,128)(2,1)} %get-tuple-element.480) | data formatting | bytes 8388608 | tf_op jit(solution)/shard_map/while | solution.py:194
  169.8 28.6 %while.36 = (s32[]{:T(128)}, f32[8,256]{1,0:T(8,128)S(1)}, f32[8,256]{1,0:T(8,128)S(1)}, f32[8,256,128]{2,1,0:T(8,128)S(1)}, s32[256]{0:T(256)S(1)}, /*index=5*/...) while((s32[]{:T(128)}, f32[8,256]{1,0:T(8,128)S(1)}, ...), condition=%wide.region_12.13_spmd, body=%wide.region_7.12_spmd.sunk | while | flops 551162368 | bytes 22160680 | solution.py:194
  169.9 0.6 slice.28
  171.0 6.0 %conditional.2 = (f32[8,256]{1,0:T(8,128)S(1)}, f32[8,256]{1,0:T(8,128)S(1)}, f32[8,256,128]{2,1,0:T(8,128)S(1)}) conditional(s32[]{:T(128)} %convert_element_type.129, (s32[]{:T(128)}, s32[512]{0:T(512)S(1)}, s32[256]{0:T(256)S(1)}, bf16[2048,1024]{0,1:T(8,128)(2,1)}, bf16[256,8,128]{2,0,1:T(8,128)(2,1)S(1)}, /*index=5*/f32[8,256]{1,0:T(8,128)S(1)}, ...), branch_computations={%region_8.10_spmd, %region_11.11_spmd} | conditional | flops 551162368 | bytes 22142018 | solution.py:107
  171.0 1.7 constant_dynamic-slice_fusion
  172.9 0.9 fusion
  173.8 1.0 fusion.2
  174.8 2.1 %fusion.6 = f32[8,256,128]{2,1,0:T(8,128)S(1)} fusion(bf16[512,8,128]{0,2,1:T(8,128)(2,1)S(1)} %bitcast.91, f32[8,512,256]{2,1,0:T(8,128)S(1)} %get-tuple-element.477, f32[8,256]{1,0:T(8,128)S(1)} %max.5, pred[256,512]{0,1:T(8,128)(4,1)S(1)} %broadcast_compare_fusion, f32[8,256,128]{2,1,0:T(8,128)S(1)} %get-tuple-element.364, ...), kind=kOutput, calls=%fused_computation.7 | convolution fusion | flops 274202624 | bytes 7487488 | tf_op jit(solution)/shard_map/while/body/eval_jaxpr/cond/branch_0_fun/hqk,khd->hqd/dot_general | solution.py:100
  177.0 0.6 slice.28
  178.1 6.0 %conditional.2 = (f32[8,256]{1,0:T(8,128)S(1)}, f32[8,256]{1,0:T(8,128)S(1)}, f32[8,256,128]{2,1,0:T(8,128)S(1)}) conditional(s32[]{:T(128)} %convert_element_type.129, (s32[]{:T(128)}, s32[512]{0:T(512)S(1)}, s32[256]{0:T(256)S(1)}, bf16[2048,1024]{0,1:T(8,128)(2,1)}, bf16[256,8,128]{2,0,1:T(8,128)(2,1)S(1)}, /*index=5*/f32[8,256]{1,0:T(8,128)S(1)}, ...), branch_computations={%region_8.10_spmd, %region_11.11_spmd} | conditional | flops 551162368 | bytes 22142018 | solution.py:107
  178.1 1.7 constant_dynamic-slice_fusion
  180.0 0.9 fusion
  180.9 1.0 fusion.2
  182.0 2.1 %fusion.6 = f32[8,256,128]{2,1,0:T(8,128)S(1)} fusion(bf16[512,8,128]{0,2,1:T(8,128)(2,1)S(1)} %bitcast.91, f32[8,512,256]{2,1,0:T(8,128)S(1)} %get-tuple-element.477, f32[8,256]{1,0:T(8,128)S(1)} %max.5, pred[256,512]{0,1:T(8,128)(4,1)S(1)} %broadcast_compare_fusion, f32[8,256,128]{2,1,0:T(8,128)S(1)} %get-tuple-element.364, ...), kind=kOutput, calls=%fused_computation.7 | convolution fusion | flops 274202624 | bytes 7487488 | tf_op jit(solution)/shard_map/while/body/eval_jaxpr/cond/branch_0_fun/hqk,khd->hqd/dot_general | solution.py:100
  184.1 0.6 slice.28
  185.3 6.0 %conditional.2 = (f32[8,256]{1,0:T(8,128)S(1)}, f32[8,256]{1,0:T(8,128)S(1)}, f32[8,256,128]{2,1,0:T(8,128)S(1)}) conditional(s32[]{:T(128)} %convert_element_type.129, (s32[]{:T(128)}, s32[512]{0:T(512)S(1)}, s32[256]{0:T(256)S(1)}, bf16[2048,1024]{0,1:T(8,128)(2,1)}, bf16[256,8,128]{2,0,1:T(8,128)(2,1)S(1)}, /*index=5*/f32[8,256]{1,0:T(8,128)S(1)}, ...), branch_computations={%region_8.10_spmd, %region_11.11_spmd} | conditional | flops 551162368 | bytes 22142018 | solution.py:107
  185.3 1.7 constant_dynamic-slice_fusion
  187.1 0.9 fusion
  188.1 1.0 fusion.2
  189.1 2.1 %fusion.6 = f32[8,256,128]{2,1,0:T(8,128)S(1)} fusion(bf16[512,8,128]{0,2,1:T(8,128)(2,1)S(1)} %bitcast.91, f32[8,512,256]{2,1,0:T(8,128)S(1)} %get-tuple-element.477, f32[8,256]{1,0:T(8,128)S(1)} %max.5, pred[256,512]{0,1:T(8,128)(4,1)S(1)} %broadcast_compare_fusion, f32[8,256,128]{2,1,0:T(8,128)S(1)} %get-tuple-element.364, ...), kind=kOutput, calls=%fused_computation.7 | convolution fusion | flops 274202624 | bytes 7487488 | tf_op jit(solution)/shard_map/while/body/eval_jaxpr/cond/branch_0_fun/hqk,khd->hqd/dot_general | solution.py:100
  191.3 0.6 slice.28
  192.4 6.0 %conditional.2 = (f32[8,256]{1,0:T(8,128)S(1)}, f32[8,256]{1,0:T(8,128)S(1)}, f32[8,256,128]{2,1,0:T(8,128)S(1)}) conditional(s32[]{:T(128)} %convert_element_type.129, (s32[]{:T(128)}, s32[512]{0:T(512)S(1)}, s32[256]{0:T(256)S(1)}, bf16[2048,1024]{0,1:T(8,128)(2,1)}, bf16[256,8,128]{2,0,1:T(8,128)(2,1)S(1)}, /*index=5*/f32[8,256]{1,0:T(8,128)S(1)}, ...), branch_computations={%region_8.10_spmd, %region_11.11_spmd} | conditional | flops 551162368 | bytes 22142018 | solution.py:107
  192.4 1.7 constant_dynamic-slice_fusion
  194.3 0.9 fusion
  195.2 1.0 fusion.2
  196.2 2.1 %fusion.6 = f32[8,256,128]{2,1,0:T(8,128)S(1)} fusion(bf16[512,8,128]{0,2,1:T(8,128)(2,1)S(1)} %bitcast.91, f32[8,512,256]{2,1,0:T(8,128)S(1)} %get-tuple-element.477, f32[8,256]{1,0:T(8,128)S(1)} %max.5, pred[256,512]{0,1:T(8,128)(4,1)S(1)} %broadcast_compare_fusion, f32[8,256,128]{2,1,0:T(8,128)S(1)} %get-tuple-element.364, ...), kind=kOutput, calls=%fused_computation.7 | convolution fusion | flops 274202624 | bytes 7487488 | tf_op jit(solution)/shard_map/while/body/eval_jaxpr/cond/branch_0_fun/hqk,khd->hqd/dot_general | solution.py:100
  198.4 1.1 copy_bitcast_fusion
  (78 shorter events, 4.7 us)
Async XLA Ops:
  7.2 21.9 %copy-start = (bf16[256,128]{1,0:T(8,128)(2,1)S(1)}, bf16[256,128]{1,0:T(8,128)(2,1)}, u32[]{:S(2)}) copy-start(bf16[256,128]{1,0:T(8,128)(2,1)} %param.19) | copy-start | bytes 196612
  7.2 35.6 %all-gather.7.cloned.1.call-start = ((), (), s32[]{:S(2)}) async-start(), calls=%async_computation.1 | async-start | bytes 2359296 | tf_op jit(solution)/shard_map/all_gather | solution.py:24
  13.4 137.4 %all-gather.5.cloned.1.call-start = ((), (), s32[]{:S(2)}) async-start(), calls=%async_computation | async-start | bytes 9437184 | tf_op jit(solution)/shard_map/all_gather | solution.py:15
  42.8 13.6 %copy-start.6 = (f32[16]{0:T(128)S(1)}, f32[16]{0:T(128)}, u32[]{:S(2)}) copy-start(f32[16]{0:T(128)} %param.22) | copy-start | bytes 196
  56.4 3.8 %copy-start.1 = (bf16[256,1024]{1,0:T(8,128)(2,1)S(1)}, bf16[256,1024]{1,0:T(8,128)(2,1)}, u32[]{:S(2)}) copy-start(bf16[256,1024]{1,0:T(8,128)(2,1)} %param.17) | copy-start | bytes 1572868
  56.4 12.1 %copy-start.5 = (f32[1024]{0:T(1024)S(1)}, f32[1024]{0:T(1024)}, u32[]{:S(2)}) copy-start(f32[1024]{0:T(1024)} %param.23) | copy-start | bytes 12292
  58.5 10.4 %copy-start.4 = (bf16[256,1024]{1,0:T(8,128)(2,1)S(1)}, bf16[256,1024]{1,0:T(8,128)(2,1)}, u32[]{:S(2)}) copy-start(bf16[256,1024]{1,0:T(8,128)(2,1)} %param.25) | copy-start | bytes 1572868
  58.5 11.7 %copy-start.3 = (bf16[256,1024]{1,0:T(8,128)(2,1)S(1)}, bf16[256,1024]{1,0:T(8,128)(2,1)}, u32[]{:S(2)}) copy-start(bf16[256,1024]{1,0:T(8,128)(2,1)} %param.24) | copy-start | bytes 1572868
  68.9 87.8 %copy-start.2 = (bf16[256,1024]{1,0:T(8,128)(2,1)}, bf16[256,1024]{1,0:T(8,128)(2,1)S(1)}, u32[]{:S(2)}) copy-start(bf16[256,1024]{1,0:T(8,128)(2,1)S(1)} %multiply_convert_fusion) | copy-start | bytes 1572868
Sparse Core Ops, SparseCore 0:
  13.6 29.2 all-gather.6
  70.3 80.4 all-gather.4
